TPU v7x, 512 devices: a whole 4x8x8 slice. The times are simulated.
512 devices in a mesh: cuts: 8 (over y), row: 64 (over x, z, core).
Axes of the slice: x: 4, y: 8, z: 8, core: 2. Of those that a mesh axis runs over, the one named last changes fastest.
Arguments:
- block_tiles: float32 [192, 24, 128, 128], P('row'), may hold values from -0.109375 to 0.109375
- tile_pattern: int32 [192, 24], P('row'), may hold values from 0 to 191, as said below
- start_vectors: float32 [8, 32, 24576], P('cuts', None, 'row'), may hold values from -8 to 8
- centers: float32 [8], P('cuts'), may hold values from -0.3 to 0.3
- halfwidths: float32 [8], P('cuts'), may hold values from 0.9 to 1.3
- dup_pairs: int32 [8, 8, 2], P('cuts'), may hold values from 0 to 31, as said below
Outputs:
- filtered_basis: float32 [8, 32, 24576], P('cuts', None, 'row')
- projected: float32 [8, 32, 32], P('cuts')
Inputs may be any that keep to these rules, and one draw needn't show every extreme that they name: tile_pattern[r, 0] = r; the other entries of block row r are distinct block rows, each within 12 of r cyclically and different from r. `dup_pairs`: within one slice the first entries of the pairs are distinct, and so are the second entries; the pairs of slice 0 are not used.
All inputs are finite; a program needn't handle non-finite values.
Results may differ from a plain program's by a relative error of at most 0.00015.
Values sent between devices are 32-bit elements; how exact they have to be, the bound alone decides.
A program may use at most 64 MiB of HBM per device.

v0:
```python
import math
import jax
import jax.numpy as jnp
from jax import lax
from jax.sharding import PartitionSpec as P

DEG = 8
REACH = 12


def from_behind(shard, axis, by):
    size = lax.axis_size(axis)
    return lax.ppermute(shard, axis, [(i, (i + by) % size) for i in range(size)])


def from_behind_2(value, axis, steps):
    count = lax.axis_size(axis)
    leading, last = (max(0, -steps), min(count, count - steps))
    return lax.ppermute(value, axis, [(source, source + steps) for source in range(leading, last)])


def apply_local(vectors, block_tiles, tile_pattern):
    vec_count = vectors.shape[0]
    local_rows = block_tiles.shape[0]
    tile_width = block_tiles.shape[2]
    device_reach = (REACH + local_rows - 1) // local_rows
    pieces = []
    for offset in range(-device_reach, device_reach + 1):
        if offset == 0:
            pieces.append(vectors)
        else:
            pieces.append(from_behind(vectors, "row", -offset))
    extended = jnp.concatenate(pieces, axis=1).reshape(
        vec_count, len(pieces) * local_rows, tile_width
    )
    total_rows = local_rows * lax.axis_size("row")
    lowest = (lax.axis_index("row") - device_reach) * local_rows
    positions = (tile_pattern - lowest) % total_rows
    picked = jnp.take(extended, positions, axis=1)
    product = jnp.einsum("vrkc,rkdc->vrd", picked, block_tiles, precision=lax.Precision.HIGHEST)
    return product.reshape(vec_count, local_rows * tile_width)


def lower_solve(factor, right_side):
    return lax.linalg.triangular_solve(factor, right_side, left_side=True, lower=True)


def local(block_tiles, tile_pattern, start_vectors, centers, halfwidths, dup_pairs):
    initial = start_vectors[0]
    center = centers[0]
    halfwidth = halfwidths[0]
    order_total = initial.shape[1] * lax.axis_size("row")
    previous = initial
    current = (apply_local(initial, block_tiles, tile_pattern) - center * initial) / halfwidth
    for degree in range(DEG - 1):
        following = (
            2.0 * (apply_local(current, block_tiles, tile_pattern) - center * current) / halfwidth
            - previous
        )
        previous, current = (current, following)
    gram_matrix = lax.psum(jnp.dot(current, current.T, precision=lax.Precision.HIGHEST), "row")
    factor = jnp.linalg.cholesky(gram_matrix)
    basis_raw = math.sqrt(order_total) * lower_solve(factor, current)
    imaged = apply_local(basis_raw, block_tiles, tile_pattern)
    projected = (
        lax.psum(jnp.dot(basis_raw, imaged.T, precision=lax.Precision.HIGHEST), "row") / order_total
    )
    vec_count = basis_raw.shape[0]
    columns = jnp.arange(vec_count, dtype=jnp.int32)
    own_index = dup_pairs[0, :, 0]
    their_index = dup_pairs[0, :, 1]
    target_mask = (own_index[:, None] == columns[None, :]).astype(jnp.float32)
    lower_basis = from_behind_2(basis_raw, "cuts", 1)
    selector = (their_index[:, None] == columns[None, :]).astype(jnp.float32)
    lower_rows = jnp.dot(selector, lower_basis, precision=lax.Precision.HIGHEST)
    correlation = (
        lax.psum(jnp.dot(lower_rows, basis_raw.T, precision=lax.Precision.HIGHEST), "row")
        / order_total
    )
    filtered_basis = basis_raw - jnp.dot(
        (target_mask * correlation).T, lower_rows, precision=lax.Precision.HIGHEST
    )
    return (filtered_basis[None], projected[None])


def solution(mesh):
    in_specs = (
        P("row", None, None, None),
        P("row", None),
        P("cuts", None, "row"),
        P("cuts"),
        P("cuts"),
        P("cuts", None, None),
    )
    out_specs = (P("cuts", None, "row"), P("cuts", None, None))
    return jax.shard_map(local, mesh=mesh, in_specs=in_specs, out_specs=out_specs, check_vma=False)
```

profile of v0, /device:TPU:32, one launch (start us, length us, event | category | flops | bytes accessed | tf_op | source)
XLA Modules:
  0.0 861.8 jit_solution(17012417078433444619)
XLA Ops:
  0.6 6.1 collective-permute-start
  6.7 3.4 collective-permute-start.1
  10.2 5.5 collective-permute-start.2
  15.7 3.5 collective-permute-start.3
  19.2 5.4 collective-permute-start.4
  31.8 5.5 collective-permute-start.7
  40.6 6.7 fusion.16
  47.3 4.9 collective-permute-start.8
  58.4 6.5 collective-permute-start.12
  65.0 3.9 collective-permute-start.13
  71.7 3.7 collective-permute-start.15
  75.6 3.8 collective-permute-done.15
  80.1 6.7 fusion.14
  96.0 6.7 collective-permute-start.20
  102.8 3.5 collective-permute-start.21
  106.3 2.8 collective-permute-start.22
  109.2 5.1 collective-permute-start.23
  114.4 3.0 collective-permute-done.23
  118.2 6.7 fusion.12
  133.3 6.8 collective-permute-start.28
  140.1 3.9 collective-permute-start.29
  146.8 5.6 collective-permute-start.31
  155.4 6.7 fusion.10
  171.2 6.6 collective-permute-start.36
  177.8 3.6 collective-permute-start.37
  181.4 2.8 collective-permute-start.38
  184.3 6.1 collective-permute-start.39
  193.2 6.7 fusion.8
  208.7 6.6 collective-permute-start.44
  215.3 3.7 collective-permute-start.45
  221.9 6.0 collective-permute-start.47
  230.7 6.7 fusion.6
  246.5 6.6 collective-permute-start.52
  253.1 3.5 collective-permute-start.53
  259.5 6.0 collective-permute-start.55
  268.5 6.7 fusion.4
  284.1 6.6 collective-permute-start.60
  290.7 3.6 collective-permute-start.61
  297.1 6.0 collective-permute-start.63
  306.1 7.2 fusion.43
  313.5 250.9 %psum.21 = f32[32,32]{0,1:T(8,128)S(1)} all-reduce(f32[32,32]{0,1:T(8,128)S(1)} %convolution_bitcast_fusion), channel_id=1, replica_groups=mesh['cuts'=8,'row'=64] {'row'}, use_global_device_ids=true, to_apply=%region_0.2 | all-reduce | flops 1024 | bytes 8192 | tf_op jit(solution)/shard_map/psum | solution.py:61
  564.5 2.9 cholesky.16
  579.2 7.0 collective-permute-start.69
  586.2 3.9 collective-permute-start.70
  590.1 2.9 collective-permute-start.71
  593.1 5.9 collective-permute-start.72
  602.4 6.7 fusion.30
  609.7 250.6 %all-reduce = (f32[8,32]{1,0:T(8,128)S(1)}, f32[32,32]{1,0:T(8,128)S(1)}) all-reduce(f32[8,32]{1,0:T(8,128)S(1)} %fusion.129, f32[32,32]{1,0:T(8,128)S(1)} %fusion.64), channel_id=1, replica_groups=mesh['cuts'=8,'row'=64] {'row'}, use_global_device_ids=true, to_apply=%region_3.5 | all-reduce | flops 1280 | bytes 10240 | tf_op jit(solution)/shard_map/psum | solution.py:77
  (237 shorter events, 115.5 us)
Async XLA Ops:
  0.6 26.9 %collective-permute-start = (f32[32,384]{1,0:T(8,128)}, f32[32,384]{1,0:T(8,128)S(1)}, u32[]{:S(2)}, u32[]{:S(2)}) collective-permute-start(f32[32,384]{1,0:T(8,128)} %bitcast.384), channel_id=1, source_target_pairs={{0,4},{1,5},{2,6},{3,7},{4,8},{5,9},{6,10},{7,11},{8,12},{9,13},{1... | collective-permute-start | bytes 147464 | tf_op jit(solution)/shard_map/ppermute | solution.py:13
  6.7 23.1 %collective-permute-start.1 = (f32[32,384]{1,0:T(8,128)}, f32[32,384]{1,0:T(8,128)S(1)}, u32[]{:S(2)}, u32[]{:S(2)}) collective-permute-start(f32[32,384]{1,0:T(8,128)} %bitcast.385), channel_id=1, source_target_pairs={{0,3},{1,4},{2,5},{3,6},{4,7},{5,8},{6,9},{7,10},{8,11},{9,12},{10... | collective-permute-start | bytes 147464 | tf_op jit(solution)/shard_map/ppermute | solution.py:13
  10.2 21.6 %collective-permute-start.2 = (f32[32,384]{1,0:T(8,128)}, f32[32,384]{1,0:T(8,128)S(1)}, u32[]{:S(2)}, u32[]{:S(2)}) collective-permute-start(f32[32,384]{1,0:T(8,128)} %bitcast.386), channel_id=1, source_target_pairs={{0,2},{1,3},{2,4},{3,5},{4,6},{5,7},{6,8},{7,9},{8,10},{9,11},{10,... | collective-permute-start | bytes 147464 | tf_op jit(solution)/shard_map/ppermute | solution.py:13
  15.7 21.6 %collective-permute-start.3 = (f32[32,384]{1,0:T(8,128)}, f32[32,384]{1,0:T(8,128)S(1)}, u32[]{:S(2)}, u32[]{:S(2)}) collective-permute-start(f32[32,384]{1,0:T(8,128)} %bitcast.387), channel_id=1, source_target_pairs={{0,1},{1,2},{2,3},{3,4},{4,5},{5,6},{6,7},{7,8},{8,9},{9,10},{10,1... | collective-permute-start | bytes 147464 | tf_op jit(solution)/shard_map/ppermute | solution.py:13
  19.2 18.1 %collective-permute-start.4 = (f32[32,384]{1,0:T(8,128)}, f32[32,384]{1,0:T(8,128)S(1)}, u32[]{:S(2)}, u32[]{:S(2)}) collective-permute-start(f32[32,384]{1,0:T(8,128)} %bitcast.388), channel_id=1, source_target_pairs={{0,63},{1,0},{2,1},{3,2},{4,3},{5,4},{6,5},{7,6},{8,7},{9,8},{10,9... | collective-permute-start | bytes 147464 | tf_op jit(solution)/shard_map/ppermute | solution.py:13
  47.3 17.7 %collective-permute-start.8 = (f32[32,384]{1,0:T(8,128)S(1)}, f32[32,384]{1,0:T(8,128)S(1)}, u32[]{:S(2)}, u32[]{:S(2)}) collective-permute-start(f32[32,384]{1,0:T(8,128)S(1)} %fusion.87), channel_id=1, source_target_pairs={{0,4},{1,5},{2,6},{3,7},{4,8},{5,9},{6,10},{7,11},{8,12},{9,13},{1... | collective-permute-start | bytes 147464 | tf_op jit(solution)/shard_map/ppermute | solution.py:13
  52.2 16.7 %collective-permute-start.9 = (f32[32,384]{1,0:T(8,128)S(1)}, f32[32,384]{1,0:T(8,128)S(1)}, u32[]{:S(2)}, u32[]{:S(2)}) collective-permute-start(f32[32,384]{1,0:T(8,128)S(1)} %fusion.87), channel_id=1, source_target_pairs={{0,3},{1,4},{2,5},{3,6},{4,7},{5,8},{6,9},{7,10},{8,11},{9,12},{10... | collective-permute-start | bytes 147464 | tf_op jit(solution)/shard_map/ppermute | solution.py:13
  54.1 17.6 %collective-permute-start.10 = (f32[32,384]{1,0:T(8,128)S(1)}, f32[32,384]{1,0:T(8,128)S(1)}, u32[]{:S(2)}, u32[]{:S(2)}) collective-permute-start(f32[32,384]{1,0:T(8,128)S(1)} %fusion.87), channel_id=1, source_target_pairs={{0,2},{1,3},{2,4},{3,5},{4,6},{5,7},{6,8},{7,9},{8,10},{9,11},{10,... | collective-permute-start | bytes 147464 | tf_op jit(solution)/shard_map/ppermute | solution.py:13
  56.1 19.4 %collective-permute-start.11 = (f32[32,384]{1,0:T(8,128)S(1)}, f32[32,384]{1,0:T(8,128)S(1)}, u32[]{:S(2)}, u32[]{:S(2)}) collective-permute-start(f32[32,384]{1,0:T(8,128)S(1)} %fusion.87), channel_id=1, source_target_pairs={{0,1},{1,2},{2,3},{3,4},{4,5},{5,6},{6,7},{7,8},{8,9},{9,10},{10,1... | collective-permute-start | bytes 147464 | tf_op jit(solution)/shard_map/ppermute | solution.py:13
  58.4 17.1 %collective-permute-start.12 = (f32[32,384]{1,0:T(8,128)S(1)}, f32[32,384]{1,0:T(8,128)S(1)}, u32[]{:S(2)}, u32[]{:S(2)}) collective-permute-start(f32[32,384]{1,0:T(8,128)S(1)} %fusion.87), channel_id=1, source_target_pairs={{0,63},{1,0},{2,1},{3,2},{4,3},{5,4},{6,5},{7,6},{8,7},{9,8},{10,9... | collective-permute-start | bytes 147464 | tf_op jit(solution)/shard_map/ppermute | solution.py:13
  86.8 15.9 %collective-permute-start.16 = (f32[32,384]{1,0:T(8,128)S(1)}, f32[32,384]{1,0:T(8,128)S(1)}, u32[]{:S(2)}, u32[]{:S(2)}) collective-permute-start(f32[32,384]{1,0:T(8,128)S(1)} %fusion.86), channel_id=1, source_target_pairs={{0,4},{1,5},{2,6},{3,7},{4,8},{5,9},{6,10},{7,11},{8,12},{9,13},{1... | collective-permute-start | bytes 147464 | tf_op jit(solution)/shard_map/ppermute | solution.py:13
  89.6 16.7 %collective-permute-start.17 = (f32[32,384]{1,0:T(8,128)S(1)}, f32[32,384]{1,0:T(8,128)S(1)}, u32[]{:S(2)}, u32[]{:S(2)}) collective-permute-start(f32[32,384]{1,0:T(8,128)S(1)} %fusion.86), channel_id=1, source_target_pairs={{0,3},{1,4},{2,5},{3,6},{4,7},{5,8},{6,9},{7,10},{8,11},{9,12},{10... | collective-permute-start | bytes 147464 | tf_op jit(solution)/shard_map/ppermute | solution.py:13
  91.5 17.6 %collective-permute-start.18 = (f32[32,384]{1,0:T(8,128)S(1)}, f32[32,384]{1,0:T(8,128)S(1)}, u32[]{:S(2)}, u32[]{:S(2)}) collective-permute-start(f32[32,384]{1,0:T(8,128)S(1)} %fusion.86), channel_id=1, source_target_pairs={{0,2},{1,3},{2,4},{3,5},{4,6},{5,7},{6,8},{7,9},{8,10},{9,11},{10,... | collective-permute-start | bytes 147464 | tf_op jit(solution)/shard_map/ppermute | solution.py:13
  93.9 20.5 %collective-permute-start.19 = (f32[32,384]{1,0:T(8,128)S(1)}, f32[32,384]{1,0:T(8,128)S(1)}, u32[]{:S(2)}, u32[]{:S(2)}) collective-permute-start(f32[32,384]{1,0:T(8,128)S(1)} %fusion.86), channel_id=1, source_target_pairs={{0,1},{1,2},{2,3},{3,4},{4,5},{5,6},{6,7},{7,8},{8,9},{9,10},{10,1... | collective-permute-start | bytes 147464 | tf_op jit(solution)/shard_map/ppermute | solution.py:13
  96.0 18.3 %collective-permute-start.20 = (f32[32,384]{1,0:T(8,128)S(1)}, f32[32,384]{1,0:T(8,128)S(1)}, u32[]{:S(2)}, u32[]{:S(2)}) collective-permute-start(f32[32,384]{1,0:T(8,128)S(1)} %fusion.86), channel_id=1, source_target_pairs={{0,63},{1,0},{2,1},{3,2},{4,3},{5,4},{6,5},{7,6},{8,7},{9,8},{10,9... | collective-permute-start | bytes 147464 | tf_op jit(solution)/shard_map/ppermute | solution.py:13
  124.9 15.1 %collective-permute-start.24 = (f32[32,384]{1,0:T(8,128)S(1)}, f32[32,384]{1,0:T(8,128)S(1)}, u32[]{:S(2)}, u32[]{:S(2)}) collective-permute-start(f32[32,384]{1,0:T(8,128)S(1)} %fusion.83), channel_id=1, source_target_pairs={{0,4},{1,5},{2,6},{3,7},{4,8},{5,9},{6,10},{7,11},{8,12},{9,13},{1... | collective-permute-start | bytes 147464 | tf_op jit(solution)/shard_map/ppermute | solution.py:13
  127.3 16.7 %collective-permute-start.25 = (f32[32,384]{1,0:T(8,128)S(1)}, f32[32,384]{1,0:T(8,128)S(1)}, u32[]{:S(2)}, u32[]{:S(2)}) collective-permute-start(f32[32,384]{1,0:T(8,128)S(1)} %fusion.83), channel_id=1, source_target_pairs={{0,3},{1,4},{2,5},{3,6},{4,7},{5,8},{6,9},{7,10},{8,11},{9,12},{10... | collective-permute-start | bytes 147464 | tf_op jit(solution)/shard_map/ppermute | solution.py:13
  129.2 17.6 %collective-permute-start.26 = (f32[32,384]{1,0:T(8,128)S(1)}, f32[32,384]{1,0:T(8,128)S(1)}, u32[]{:S(2)}, u32[]{:S(2)}) collective-permute-start(f32[32,384]{1,0:T(8,128)S(1)} %fusion.83), channel_id=1, source_target_pairs={{0,2},{1,3},{2,4},{3,5},{4,6},{5,7},{6,8},{7,9},{8,10},{9,11},{10,... | collective-permute-start | bytes 147464 | tf_op jit(solution)/shard_map/ppermute | solution.py:13
  131.1 21.2 %collective-permute-start.27 = (f32[32,384]{1,0:T(8,128)S(1)}, f32[32,384]{1,0:T(8,128)S(1)}, u32[]{:S(2)}, u32[]{:S(2)}) collective-permute-start(f32[32,384]{1,0:T(8,128)S(1)} %fusion.83), channel_id=1, source_target_pairs={{0,1},{1,2},{2,3},{3,4},{4,5},{5,6},{6,7},{7,8},{8,9},{9,10},{10,1... | collective-permute-start | bytes 147464 | tf_op jit(solution)/shard_map/ppermute | solution.py:13
  133.3 19.2 %collective-permute-start.28 = (f32[32,384]{1,0:T(8,128)S(1)}, f32[32,384]{1,0:T(8,128)S(1)}, u32[]{:S(2)}, u32[]{:S(2)}) collective-permute-start(f32[32,384]{1,0:T(8,128)S(1)} %fusion.83), channel_id=1, source_target_pairs={{0,63},{1,0},{2,1},{3,2},{4,3},{5,4},{6,5},{7,6},{8,7},{9,8},{10,9... | collective-permute-start | bytes 147464 | tf_op jit(solution)/shard_map/ppermute | solution.py:13
  162.1 15.7 %collective-permute-start.32 = (f32[32,384]{1,0:T(8,128)S(1)}, f32[32,384]{1,0:T(8,128)S(1)}, u32[]{:S(2)}, u32[]{:S(2)}) collective-permute-start(f32[32,384]{1,0:T(8,128)S(1)} %fusion.80), channel_id=1, source_target_pairs={{0,4},{1,5},{2,6},{3,7},{4,8},{5,9},{6,10},{7,11},{8,12},{9,13},{1... | collective-permute-start | bytes 147464 | tf_op jit(solution)/shard_map/ppermute | solution.py:13
  164.7 16.7 %collective-permute-start.33 = (f32[32,384]{1,0:T(8,128)S(1)}, f32[32,384]{1,0:T(8,128)S(1)}, u32[]{:S(2)}, u32[]{:S(2)}) collective-permute-start(f32[32,384]{1,0:T(8,128)S(1)} %fusion.80), channel_id=1, source_target_pairs={{0,3},{1,4},{2,5},{3,6},{4,7},{5,8},{6,9},{7,10},{8,11},{9,12},{10... | collective-permute-start | bytes 147464 | tf_op jit(solution)/shard_map/ppermute | solution.py:13
  166.6 17.6 %collective-permute-start.34 = (f32[32,384]{1,0:T(8,128)S(1)}, f32[32,384]{1,0:T(8,128)S(1)}, u32[]{:S(2)}, u32[]{:S(2)}) collective-permute-start(f32[32,384]{1,0:T(8,128)S(1)} %fusion.80), channel_id=1, source_target_pairs={{0,2},{1,3},{2,4},{3,5},{4,6},{5,7},{6,8},{7,9},{8,10},{9,11},{10,... | collective-permute-start | bytes 147464 | tf_op jit(solution)/shard_map/ppermute | solution.py:13
  168.8 21.6 %collective-permute-start.35 = (f32[32,384]{1,0:T(8,128)S(1)}, f32[32,384]{1,0:T(8,128)S(1)}, u32[]{:S(2)}, u32[]{:S(2)}) collective-permute-start(f32[32,384]{1,0:T(8,128)S(1)} %fusion.80), channel_id=1, source_target_pairs={{0,1},{1,2},{2,3},{3,4},{4,5},{5,6},{6,7},{7,8},{8,9},{9,10},{10,1... | collective-permute-start | bytes 147464 | tf_op jit(solution)/shard_map/ppermute | solution.py:13
  171.2 19.2 %collective-permute-start.36 = (f32[32,384]{1,0:T(8,128)S(1)}, f32[32,384]{1,0:T(8,128)S(1)}, u32[]{:S(2)}, u32[]{:S(2)}) collective-permute-start(f32[32,384]{1,0:T(8,128)S(1)} %fusion.80), channel_id=1, source_target_pairs={{0,63},{1,0},{2,1},{3,2},{4,3},{5,4},{6,5},{7,6},{8,7},{9,8},{10,9... | collective-permute-start | bytes 147464 | tf_op jit(solution)/shard_map/ppermute | solution.py:13
  177.8 12.7 %collective-permute-start.37 = (f32[32,384]{1,0:T(8,128)S(1)}, f32[32,384]{1,0:T(8,128)S(1)}, u32[]{:S(2)}, u32[]{:S(2)}) collective-permute-start(f32[32,384]{1,0:T(8,128)S(1)} %fusion.80), channel_id=1, source_target_pairs={{0,62},{1,63},{2,0},{3,1},{4,2},{5,3},{6,4},{7,5},{8,6},{9,7},{10,... | collective-permute-start | bytes 147464 | tf_op jit(solution)/shard_map/ppermute | solution.py:13
  200.0 15.3 %collective-permute-start.40 = (f32[32,384]{1,0:T(8,128)S(1)}, f32[32,384]{1,0:T(8,128)S(1)}, u32[]{:S(2)}, u32[]{:S(2)}) collective-permute-start(f32[32,384]{1,0:T(8,128)S(1)} %fusion.77), channel_id=1, source_target_pairs={{0,4},{1,5},{2,6},{3,7},{4,8},{5,9},{6,10},{7,11},{8,12},{9,13},{1... | collective-permute-start | bytes 147464 | tf_op jit(solution)/shard_map/ppermute | solution.py:13
  202.3 16.7 %collective-permute-start.41 = (f32[32,384]{1,0:T(8,128)S(1)}, f32[32,384]{1,0:T(8,128)S(1)}, u32[]{:S(2)}, u32[]{:S(2)}) collective-permute-start(f32[32,384]{1,0:T(8,128)S(1)} %fusion.77), channel_id=1, source_target_pairs={{0,3},{1,4},{2,5},{3,6},{4,7},{5,8},{6,9},{7,10},{8,11},{9,12},{10... | collective-permute-start | bytes 147464 | tf_op jit(solution)/shard_map/ppermute | solution.py:13
  204.3 17.6 %collective-permute-start.42 = (f32[32,384]{1,0:T(8,128)S(1)}, f32[32,384]{1,0:T(8,128)S(1)}, u32[]{:S(2)}, u32[]{:S(2)}) collective-permute-start(f32[32,384]{1,0:T(8,128)S(1)} %fusion.77), channel_id=1, source_target_pairs={{0,2},{1,3},{2,4},{3,5},{4,6},{5,7},{6,8},{7,9},{8,10},{9,11},{10,... | collective-permute-start | bytes 147464 | tf_op jit(solution)/shard_map/ppermute | solution.py:13
  206.2 21.7 %collective-permute-start.43 = (f32[32,384]{1,0:T(8,128)S(1)}, f32[32,384]{1,0:T(8,128)S(1)}, u32[]{:S(2)}, u32[]{:S(2)}) collective-permute-start(f32[32,384]{1,0:T(8,128)S(1)} %fusion.77), channel_id=1, source_target_pairs={{0,1},{1,2},{2,3},{3,4},{4,5},{5,6},{6,7},{7,8},{8,9},{9,10},{10,1... | collective-permute-start | bytes 147464 | tf_op jit(solution)/shard_map/ppermute | solution.py:13
  208.7 19.2 %collective-permute-start.44 = (f32[32,384]{1,0:T(8,128)S(1)}, f32[32,384]{1,0:T(8,128)S(1)}, u32[]{:S(2)}, u32[]{:S(2)}) collective-permute-start(f32[32,384]{1,0:T(8,128)S(1)} %fusion.77), channel_id=1, source_target_pairs={{0,63},{1,0},{2,1},{3,2},{4,3},{5,4},{6,5},{7,6},{8,7},{9,8},{10,9... | collective-permute-start | bytes 147464 | tf_op jit(solution)/shard_map/ppermute | solution.py:13
  215.3 12.7 %collective-permute-start.45 = (f32[32,384]{1,0:T(8,128)S(1)}, f32[32,384]{1,0:T(8,128)S(1)}, u32[]{:S(2)}, u32[]{:S(2)}) collective-permute-start(f32[32,384]{1,0:T(8,128)S(1)} %fusion.77), channel_id=1, source_target_pairs={{0,62},{1,63},{2,0},{3,1},{4,2},{5,3},{6,4},{7,5},{8,6},{9,7},{10,... | collective-permute-start | bytes 147464 | tf_op jit(solution)/shard_map/ppermute | solution.py:13
  237.4 15.6 %collective-permute-start.48 = (f32[32,384]{1,0:T(8,128)S(1)}, f32[32,384]{1,0:T(8,128)S(1)}, u32[]{:S(2)}, u32[]{:S(2)}) collective-permute-start(f32[32,384]{1,0:T(8,128)S(1)} %fusion.74), channel_id=1, source_target_pairs={{0,4},{1,5},{2,6},{3,7},{4,8},{5,9},{6,10},{7,11},{8,12},{9,13},{1... | collective-permute-start | bytes 147464 | tf_op jit(solution)/shard_map/ppermute | solution.py:13
  239.9 16.7 %collective-permute-start.49 = (f32[32,384]{1,0:T(8,128)S(1)}, f32[32,384]{1,0:T(8,128)S(1)}, u32[]{:S(2)}, u32[]{:S(2)}) collective-permute-start(f32[32,384]{1,0:T(8,128)S(1)} %fusion.74), channel_id=1, source_target_pairs={{0,3},{1,4},{2,5},{3,6},{4,7},{5,8},{6,9},{7,10},{8,11},{9,12},{10... | collective-permute-start | bytes 147464 | tf_op jit(solution)/shard_map/ppermute | solution.py:13
  241.9 17.6 %collective-permute-start.50 = (f32[32,384]{1,0:T(8,128)S(1)}, f32[32,384]{1,0:T(8,128)S(1)}, u32[]{:S(2)}, u32[]{:S(2)}) collective-permute-start(f32[32,384]{1,0:T(8,128)S(1)} %fusion.74), channel_id=1, source_target_pairs={{0,2},{1,3},{2,4},{3,5},{4,6},{5,7},{6,8},{7,9},{8,10},{9,11},{10,... | collective-permute-start | bytes 147464 | tf_op jit(solution)/shard_map/ppermute | solution.py:13
  244.2 21.4 %collective-permute-start.51 = (f32[32,384]{1,0:T(8,128)S(1)}, f32[32,384]{1,0:T(8,128)S(1)}, u32[]{:S(2)}, u32[]{:S(2)}) collective-permute-start(f32[32,384]{1,0:T(8,128)S(1)} %fusion.74), channel_id=1, source_target_pairs={{0,1},{1,2},{2,3},{3,4},{4,5},{5,6},{6,7},{7,8},{8,9},{9,10},{10,1... | collective-permute-start | bytes 147464 | tf_op jit(solution)/shard_map/ppermute | solution.py:13
  246.5 19.1 %collective-permute-start.52 = (f32[32,384]{1,0:T(8,128)S(1)}, f32[32,384]{1,0:T(8,128)S(1)}, u32[]{:S(2)}, u32[]{:S(2)}) collective-permute-start(f32[32,384]{1,0:T(8,128)S(1)} %fusion.74), channel_id=1, source_target_pairs={{0,63},{1,0},{2,1},{3,2},{4,3},{5,4},{6,5},{7,6},{8,7},{9,8},{10,9... | collective-permute-start | bytes 147464 | tf_op jit(solution)/shard_map/ppermute | solution.py:13
  275.2 15.4 %collective-permute-start.56 = (f32[32,384]{1,0:T(8,128)S(1)}, f32[32,384]{1,0:T(8,128)S(1)}, u32[]{:S(2)}, u32[]{:S(2)}) collective-permute-start(f32[32,384]{1,0:T(8,128)S(1)} %fusion.71), channel_id=1, source_target_pairs={{0,4},{1,5},{2,6},{3,7},{4,8},{5,9},{6,10},{7,11},{8,12},{9,13},{1... | collective-permute-start | bytes 147464 | tf_op jit(solution)/shard_map/ppermute | solution.py:13
  277.6 16.7 %collective-permute-start.57 = (f32[32,384]{1,0:T(8,128)S(1)}, f32[32,384]{1,0:T(8,128)S(1)}, u32[]{:S(2)}, u32[]{:S(2)}) collective-permute-start(f32[32,384]{1,0:T(8,128)S(1)} %fusion.71), channel_id=1, source_target_pairs={{0,3},{1,4},{2,5},{3,6},{4,7},{5,8},{6,9},{7,10},{8,11},{9,12},{10... | collective-permute-start | bytes 147464 | tf_op jit(solution)/shard_map/ppermute | solution.py:13
  279.5 17.6 %collective-permute-start.58 = (f32[32,384]{1,0:T(8,128)S(1)}, f32[32,384]{1,0:T(8,128)S(1)}, u32[]{:S(2)}, u32[]{:S(2)}) collective-permute-start(f32[32,384]{1,0:T(8,128)S(1)} %fusion.71), channel_id=1, source_target_pairs={{0,2},{1,3},{2,4},{3,5},{4,6},{5,7},{6,8},{7,9},{8,10},{9,11},{10,... | collective-permute-start | bytes 147464 | tf_op jit(solution)/shard_map/ppermute | solution.py:13
  281.7 21.5 %collective-permute-start.59 = (f32[32,384]{1,0:T(8,128)S(1)}, f32[32,384]{1,0:T(8,128)S(1)}, u32[]{:S(2)}, u32[]{:S(2)}) collective-permute-start(f32[32,384]{1,0:T(8,128)S(1)} %fusion.71), channel_id=1, source_target_pairs={{0,1},{1,2},{2,3},{3,4},{4,5},{5,6},{6,7},{7,8},{8,9},{9,10},{10,1... | collective-permute-start | bytes 147464 | tf_op jit(solution)/shard_map/ppermute | solution.py:13
  284.1 19.1 %collective-permute-start.60 = (f32[32,384]{1,0:T(8,128)S(1)}, f32[32,384]{1,0:T(8,128)S(1)}, u32[]{:S(2)}, u32[]{:S(2)}) collective-permute-start(f32[32,384]{1,0:T(8,128)S(1)} %fusion.71), channel_id=1, source_target_pairs={{0,63},{1,0},{2,1},{3,2},{4,3},{5,4},{6,5},{7,6},{8,7},{9,8},{10,9... | collective-permute-start | bytes 147464 | tf_op jit(solution)/shard_map/ppermute | solution.py:13
  571.5 14.7 %collective-permute-start.65 = (f32[32,384]{1,0:T(8,128)S(1)}, f32[32,384]{1,0:T(8,128)S(1)}, u32[]{:S(2)}, u32[]{:S(2)}) collective-permute-start(f32[32,384]{1,0:T(8,128)S(1)} %convolution_multiply_fusion), channel_id=1, source_target_pairs={{0,4},{1,5},{2,6},{3,7},{4,8},{5,9},{6,10},{7,11},{8,12},{9,13},{1... | collective-permute-start | bytes 147464 | tf_op jit(solution)/shard_map/ppermute | solution.py:13
  573.4 16.7 %collective-permute-start.66 = (f32[32,384]{1,0:T(8,128)S(1)}, f32[32,384]{1,0:T(8,128)S(1)}, u32[]{:S(2)}, u32[]{:S(2)}) collective-permute-start(f32[32,384]{1,0:T(8,128)S(1)} %convolution_multiply_fusion), channel_id=1, source_target_pairs={{0,3},{1,4},{2,5},{3,6},{4,7},{5,8},{6,9},{7,10},{8,11},{9,12},{10... | collective-permute-start | bytes 147464 | tf_op jit(solution)/shard_map/ppermute | solution.py:13
  575.3 17.7 %collective-permute-start.67 = (f32[32,384]{1,0:T(8,128)S(1)}, f32[32,384]{1,0:T(8,128)S(1)}, u32[]{:S(2)}, u32[]{:S(2)}) collective-permute-start(f32[32,384]{1,0:T(8,128)S(1)} %convolution_multiply_fusion), channel_id=1, source_target_pairs={{0,2},{1,3},{2,4},{3,5},{4,6},{5,7},{6,8},{7,9},{8,10},{9,11},{10,... | collective-permute-start | bytes 147464 | tf_op jit(solution)/shard_map/ppermute | solution.py:13
  577.3 21.7 %collective-permute-start.68 = (f32[32,384]{1,0:T(8,128)S(1)}, f32[32,384]{1,0:T(8,128)S(1)}, u32[]{:S(2)}, u32[]{:S(2)}) collective-permute-start(f32[32,384]{1,0:T(8,128)S(1)} %convolution_multiply_fusion), channel_id=1, source_target_pairs={{0,1},{1,2},{2,3},{3,4},{4,5},{5,6},{6,7},{7,8},{8,9},{9,10},{10,1... | collective-permute-start | bytes 147464 | tf_op jit(solution)/shard_map/ppermute | solution.py:13
  579.2 22.4 %collective-permute-start.69 = (f32[32,384]{1,0:T(8,128)S(1)}, f32[32,384]{1,0:T(8,128)S(1)}, u32[]{:S(2)}, u32[]{:S(2)}) collective-permute-start(f32[32,384]{1,0:T(8,128)S(1)} %convolution_multiply_fusion), channel_id=1, source_target_pairs={{0,63},{1,0},{2,1},{3,2},{4,3},{5,4},{6,5},{7,6},{8,7},{9,8},{10,9... | collective-permute-start | bytes 147464 | tf_op jit(solution)/shard_map/ppermute | solution.py:13
  586.2 15.4 %collective-permute-start.70 = (f32[32,384]{1,0:T(8,128)S(1)}, f32[32,384]{1,0:T(8,128)S(1)}, u32[]{:S(2)}, u32[]{:S(2)}) collective-permute-start(f32[32,384]{1,0:T(8,128)S(1)} %convolution_multiply_fusion), channel_id=1, source_target_pairs={{0,62},{1,63},{2,0},{3,1},{4,2},{5,3},{6,4},{7,5},{8,6},{9,7},{10,... | collective-permute-start | bytes 147464 | tf_op jit(solution)/shard_map/ppermute | solution.py:13
  (27 other events, 505.2 us)
where the time goes:
time: 864 us; the launch traced here: 862 us
  blocking collectives  501 us (58%)
  starting transfers between devices  258 us (30%)
  matrix products  62.8 us (7%)
  waiting for transfers between devices  19.8 us (2%)
    ppermute x72, starting transfers between devices, from_behind(): lax.ppermute(shard, axis, [(i, (i + by) % size) for i in range(size)])  255 us
    psum x1, blocking collectives, local(): lax.psum(jnp.dot(current, current.T, precision=lax.Precision.HIGHEST), 'r...  251 us
    psum x1, blocking collectives, local(): lax.psum(jnp.dot(lower_rows, basis_raw.T, precision=lax.Precision.HIGHEST...  251 us
    dot_general x9, matrix products, apply_local(): jnp.einsum('vrkc,rkdc->vrd', picked, block_tiles, precision=lax.Precision...  60.9 us
    ppermute x72, waiting for transfers between devices, from_behind(): lax.ppermute(shard, axis, [(i, (i + by) % size) for i in range(size)])  19.8 us
  transfers between devices with their start and end apart: 73, of which 8 were waited for; matrix products, arithmetic and copies ran while one was open for 1% of the time, Pallas kernels for 0%

commit v1 on v0

--- a/solution.py
+++ b/solution.py
@@ -58,7 +58,13 @@
             - previous
         )
         previous, current = (current, following)
-    gram_matrix = lax.psum(jnp.dot(current, current.T, precision=lax.Precision.HIGHEST), "row")
+
+    def watch_set(arr_in):
+        aux = lax.all_gather(arr_in, axis_name="row")
+        shaped = jnp.sum(aux, axis=0)
+        return shaped
+
+    gram_matrix = watch_set(jnp.dot(current, current.T, precision=lax.Precision.HIGHEST))
     factor = jnp.linalg.cholesky(gram_matrix)
     basis_raw = math.sqrt(order_total) * lower_solve(factor, current)
     imaged = apply_local(basis_raw, block_tiles, tile_pattern)

time: 864 us -> 665 us (0.77)
  the two profiles are of different devices: /device:TPU:32 before, /device:TPU:56 now
where the time goes in v1:
time: 665 us; the launch traced here: 663 us
  blocking collectives  302 us (45%)
  starting transfers between devices  257 us (39%)
  matrix products  62.8 us (9%)
  waiting for transfers between devices  21.1 us (3%)
  other arithmetic  8.22 us (1%)
  local copies, waits for them, and re-layouts  7.77 us (1%)
    ppermute x72, starting transfers between devices, from_behind(): lax.ppermute(shard, axis, [(i, (i + by) % size) for i in range(size)])  255 us
    psum x1, blocking collectives, local(): lax.psum(jnp.dot(lower_rows, basis_raw.T, precision=lax.Precision.HIGHEST...  251 us
    dot_general x9, matrix products, apply_local(): jnp.einsum('vrkc,rkdc->vrd', picked, block_tiles, precision=lax.Precision...  60.9 us
    all_gather x1, blocking collectives, watch_set(): aux = lax.all_gather(arr_in, axis_name='row')  51.7 us
    ppermute x72, waiting for transfers between devices, from_behind(): lax.ppermute(shard, axis, [(i, (i + by) % size) for i in range(size)])  21.1 us
  transfers between devices with their start and end apart: 73, of which 9 were waited for; matrix products, arithmetic and copies ran while one was open for 1% of the time, Pallas kernels for 0%

profile of v1, /device:TPU:56, one launch (start us, length us, event | category | flops | bytes accessed | tf_op | source)
XLA Modules:
  0.0 662.6 jit_solution(6954247201528074622)
XLA Ops:
  0.6 6.1 collective-permute-start
  6.7 3.4 collective-permute-start.1
  10.2 5.5 collective-permute-start.2
  15.7 3.5 collective-permute-start.3
  19.2 5.4 collective-permute-start.4
  31.8 5.5 collective-permute-start.7
  40.6 6.7 %fusion.16 = f32[3,32,128,1]{2,1,3,0:T(8,128)S(1)} fusion(f32[3,24,128,128]{3,2,1,0:T(8,128)} %param.8, f32[3,24,32,128]{3,2,1,0:T(8,128)S(1)} %bitcast.378, pred[3,24]{1,0:T(4,128)(4,1)S(1)} %get-tuple-element.5), kind=kOutput, calls=%fused_computation.25 | convolution fusion | flops 453279744 | bytes 5947464 | tf_op jit(solution)/shard_map/vrkc,rkdc->vrd/dot_general | solution.py:40
  47.3 4.9 collective-permute-start.8
  58.4 6.5 collective-permute-start.12
  65.0 3.9 collective-permute-start.13
  71.7 3.7 collective-permute-start.15
  75.6 3.8 collective-permute-done.15
  80.1 6.7 %fusion.14 = f32[3,32,128,1]{2,1,3,0:T(8,128)S(1)} fusion(f32[3,24,128,128]{3,2,1,0:T(8,128)} %param.8, f32[3,24,32,128]{3,2,1,0:T(8,128)S(1)} %bitcast.379, pred[3,24]{1,0:T(4,128)(4,1)S(1)} %get-tuple-element.5), kind=kOutput, calls=%fused_computation.23 | convolution fusion | flops 453279744 | bytes 5947464 | tf_op jit(solution)/shard_map/vrkc,rkdc->vrd/dot_general | solution.py:40
  96.0 6.7 %collective-permute-start.20 = (f32[32,384]{1,0:T(8,128)S(1)}, f32[32,384]{1,0:T(8,128)S(1)}, u32[]{:S(2)}, u32[]{:S(2)}) collective-permute-start(f32[32,384]{1,0:T(8,128)S(1)} %fusion.86), channel_id=1, source_target_pairs={{0,63},{1,0},{2,1},{3,2},{4,3},{5,4},{6,5},{7,6},{8,7},{9,8},{10,9... | collective-permute-start | bytes 147464 | tf_op jit(solution)/shard_map/ppermute | solution.py:13
  102.8 3.5 collective-permute-start.21
  106.3 2.8 collective-permute-start.22
  109.2 5.1 collective-permute-start.23
  114.4 3.0 collective-permute-done.23
  118.2 6.7 %fusion.12 = f32[3,32,128,1]{2,1,3,0:T(8,128)S(1)} fusion(f32[3,24,128,128]{3,2,1,0:T(8,128)} %param.8, f32[3,24,32,128]{3,2,1,0:T(8,128)S(1)} %bitcast.380, pred[3,24]{1,0:T(4,128)(4,1)S(1)} %get-tuple-element.5), kind=kOutput, calls=%fused_computation.21 | convolution fusion | flops 453279744 | bytes 5947464 | tf_op jit(solution)/shard_map/vrkc,rkdc->vrd/dot_general | solution.py:40
  133.3 6.8 %collective-permute-start.28 = (f32[32,384]{1,0:T(8,128)S(1)}, f32[32,384]{1,0:T(8,128)S(1)}, u32[]{:S(2)}, u32[]{:S(2)}) collective-permute-start(f32[32,384]{1,0:T(8,128)S(1)} %fusion.83), channel_id=1, source_target_pairs={{0,63},{1,0},{2,1},{3,2},{4,3},{5,4},{6,5},{7,6},{8,7},{9,8},{10,9... | collective-permute-start | bytes 147464 | tf_op jit(solution)/shard_map/ppermute | solution.py:13
  140.0 3.9 collective-permute-start.29
  146.8 5.6 collective-permute-start.31
  155.4 6.7 %fusion.10 = f32[3,32,128,1]{2,1,3,0:T(8,128)S(1)} fusion(f32[3,24,128,128]{3,2,1,0:T(8,128)} %param.8, f32[3,24,32,128]{3,2,1,0:T(8,128)S(1)} %bitcast.381, pred[3,24]{1,0:T(4,128)(4,1)S(1)} %get-tuple-element.5), kind=kOutput, calls=%fused_computation.19 | convolution fusion | flops 453279744 | bytes 5947464 | tf_op jit(solution)/shard_map/vrkc,rkdc->vrd/dot_general | solution.py:40
  171.2 6.6 collective-permute-start.36
  177.8 3.6 collective-permute-start.37
  181.4 2.8 collective-permute-start.38
  184.3 6.1 collective-permute-start.39
  193.2 6.7 %fusion.8 = f32[3,32,128,1]{2,1,3,0:T(8,128)S(1)} fusion(f32[3,24,128,128]{3,2,1,0:T(8,128)} %param.8, f32[3,24,32,128]{3,2,1,0:T(8,128)S(1)} %bitcast.382, pred[3,24]{1,0:T(4,128)(4,1)S(1)} %get-tuple-element.5), kind=kOutput, calls=%fused_computation.17 | convolution fusion | flops 453279744 | bytes 5947464 | tf_op jit(solution)/shard_map/vrkc,rkdc->vrd/dot_general | solution.py:40
  208.7 6.6 collective-permute-start.44
  215.3 3.7 collective-permute-start.45
  221.9 6.0 collective-permute-start.47
  230.7 6.7 %fusion.6 = f32[3,32,128,1]{2,1,3,0:T(8,128)S(1)} fusion(f32[3,24,128,128]{3,2,1,0:T(8,128)} %param.8, f32[3,24,32,128]{3,2,1,0:T(8,128)S(1)} %bitcast.383, pred[3,24]{1,0:T(4,128)(4,1)S(1)} %get-tuple-element.5), kind=kOutput, calls=%fused_computation.15 | convolution fusion | flops 453279744 | bytes 5947464 | tf_op jit(solution)/shard_map/vrkc,rkdc->vrd/dot_general | solution.py:40
  246.5 6.6 collective-permute-start.52
  253.1 3.5 collective-permute-start.53
  256.6 2.8 collective-permute-start.54
  259.5 6.0 collective-permute-start.55
  268.5 6.7 %fusion.4 = f32[3,32,128,1]{2,1,3,0:T(8,128)S(1)} fusion(f32[3,24,128,128]{3,2,1,0:T(8,128)} %param.8, f32[3,24,32,128]{3,2,1,0:T(8,128)S(1)} %bitcast.384, pred[3,24]{1,0:T(4,128)(4,1)S(1)} %get-tuple-element.5), kind=kOutput, calls=%fused_computation.13 | convolution fusion | flops 453279744 | bytes 5947464 | tf_op jit(solution)/shard_map/vrkc,rkdc->vrd/dot_general | solution.py:40
  284.1 6.6 collective-permute-start.60
  290.7 3.7 collective-permute-start.61
  297.1 6.0 collective-permute-start.63
  306.1 7.2 %fusion.43 = f32[32,3,128]{2,0,1:T(8,128)S(1)} fusion(f32[3,24,128,128]{3,2,1,0:T(8,128)} %param.8, f32[3,24,32,128]{3,2,1,0:T(8,128)S(1)} %bitcast.376, pred[3,24]{1,0:T(4,128)(4,1)S(1)} %get-tuple-element.5, f32[3,32,128,1]{2,1,3,0:T(8,128)S(1)} %fusion.4, f32[3,32,128,1]{2,1,3,0:T(8,128)S(1)} %fusion.6, f32[3,32,128,1]{2,1,3,0:T(8,128)S(1)} %fusion.8, ...), kind=kOutput, calls=%fused_computation.44 | convolution fusion | flops 453746688 | bytes 6340688 | tf_op jit(solution)/shard_map/vrkc,rkdc->vrd/dot_general | solution.py:40
  313.5 51.7 %all-gather = f32[2048,32]{1,0:T(8,128)S(1)} all-gather(f32[32,32]{1,0:T(8,128)S(1)} %convolution_bitcast_fusion), channel_id=2, replica_groups=mesh['cuts'=8,'row'=64] {'row'}, dimensions={0}, use_global_device_ids=true | all-gather | bytes 266240 | tf_op jit(solution)/shard_map/all_gather | solution.py:63
  365.4 2.9 cholesky.16
  376.6 4.7 collective-permute-start.67
  383.2 7.0 %collective-permute-start.69 = (f32[32,384]{1,0:T(8,128)S(1)}, f32[32,384]{1,0:T(8,128)S(1)}, u32[]{:S(2)}, u32[]{:S(2)}) collective-permute-start(f32[32,384]{1,0:T(8,128)S(1)} %convolution_multiply_fusion), channel_id=1, source_target_pairs={{0,63},{1,0},{2,1},{3,2},{4,3},{5,4},{6,5},{7,6},{8,7},{9,8},{10,9... | collective-permute-start | bytes 147464 | tf_op jit(solution)/shard_map/ppermute | solution.py:13
  394.1 5.7 collective-permute-start.72
  403.3 6.7 %fusion.30 = f32[3,4,8,128]{3,2,1,0:T(8,128)S(1)} fusion(f32[3,24,128,128]{3,2,1,0:T(8,128)} %param.8, f32[3,24,32,128]{3,2,1,0:T(8,128)S(1)} %bitcast.377, pred[3,24]{1,0:T(4,128)(4,1)S(1)} %get-tuple-element.5), kind=kOutput, calls=%fused_computation.37 | convolution fusion | flops 453279744 | bytes 5947464 | tf_op jit(solution)/shard_map/vrkc,rkdc->vrd/dot_general | solution.py:40
  410.5 250.5 %all-reduce = (f32[8,32]{1,0:T(8,128)S(1)}, f32[32,32]{1,0:T(8,128)S(1)}) all-reduce(f32[8,32]{1,0:T(8,128)S(1)} %fusion.129, f32[32,32]{1,0:T(8,128)S(1)} %fusion.64), channel_id=1, replica_groups=mesh['cuts'=8,'row'=64] {'row'}, use_global_device_ids=true, to_apply=%region_3.5 | all-reduce | flops 1280 | bytes 10240 | tf_op jit(solution)/shard_map/psum | solution.py:83
  (238 shorter events, 115.0 us)
Async XLA Ops:
  0.6 26.9 %collective-permute-start = (f32[32,384]{1,0:T(8,128)}, f32[32,384]{1,0:T(8,128)S(1)}, u32[]{:S(2)}, u32[]{:S(2)}) collective-permute-start(f32[32,384]{1,0:T(8,128)} %bitcast.386), channel_id=1, source_target_pairs={{0,4},{1,5},{2,6},{3,7},{4,8},{5,9},{6,10},{7,11},{8,12},{9,13},{1... | collective-permute-start | bytes 147464 | tf_op jit(solution)/shard_map/ppermute | solution.py:13
  6.7 23.1 %collective-permute-start.1 = (f32[32,384]{1,0:T(8,128)}, f32[32,384]{1,0:T(8,128)S(1)}, u32[]{:S(2)}, u32[]{:S(2)}) collective-permute-start(f32[32,384]{1,0:T(8,128)} %bitcast.387), channel_id=1, source_target_pairs={{0,3},{1,4},{2,5},{3,6},{4,7},{5,8},{6,9},{7,10},{8,11},{9,12},{10... | collective-permute-start | bytes 147464 | tf_op jit(solution)/shard_map/ppermute | solution.py:13
  10.2 21.6 %collective-permute-start.2 = (f32[32,384]{1,0:T(8,128)}, f32[32,384]{1,0:T(8,128)S(1)}, u32[]{:S(2)}, u32[]{:S(2)}) collective-permute-start(f32[32,384]{1,0:T(8,128)} %bitcast.388), channel_id=1, source_target_pairs={{0,2},{1,3},{2,4},{3,5},{4,6},{5,7},{6,8},{7,9},{8,10},{9,11},{10,... | collective-permute-start | bytes 147464 | tf_op jit(solution)/shard_map/ppermute | solution.py:13
  15.7 21.6 %collective-permute-start.3 = (f32[32,384]{1,0:T(8,128)}, f32[32,384]{1,0:T(8,128)S(1)}, u32[]{:S(2)}, u32[]{:S(2)}) collective-permute-start(f32[32,384]{1,0:T(8,128)} %bitcast.389), channel_id=1, source_target_pairs={{0,1},{1,2},{2,3},{3,4},{4,5},{5,6},{6,7},{7,8},{8,9},{9,10},{10,1... | collective-permute-start | bytes 147464 | tf_op jit(solution)/shard_map/ppermute | solution.py:13
  19.2 18.1 %collective-permute-start.4 = (f32[32,384]{1,0:T(8,128)}, f32[32,384]{1,0:T(8,128)S(1)}, u32[]{:S(2)}, u32[]{:S(2)}) collective-permute-start(f32[32,384]{1,0:T(8,128)} %bitcast.390), channel_id=1, source_target_pairs={{0,63},{1,0},{2,1},{3,2},{4,3},{5,4},{6,5},{7,6},{8,7},{9,8},{10,9... | collective-permute-start | bytes 147464 | tf_op jit(solution)/shard_map/ppermute | solution.py:13
  47.3 17.7 %collective-permute-start.8 = (f32[32,384]{1,0:T(8,128)S(1)}, f32[32,384]{1,0:T(8,128)S(1)}, u32[]{:S(2)}, u32[]{:S(2)}) collective-permute-start(f32[32,384]{1,0:T(8,128)S(1)} %fusion.87), channel_id=1, source_target_pairs={{0,4},{1,5},{2,6},{3,7},{4,8},{5,9},{6,10},{7,11},{8,12},{9,13},{1... | collective-permute-start | bytes 147464 | tf_op jit(solution)/shard_map/ppermute | solution.py:13
  52.2 16.7 %collective-permute-start.9 = (f32[32,384]{1,0:T(8,128)S(1)}, f32[32,384]{1,0:T(8,128)S(1)}, u32[]{:S(2)}, u32[]{:S(2)}) collective-permute-start(f32[32,384]{1,0:T(8,128)S(1)} %fusion.87), channel_id=1, source_target_pairs={{0,3},{1,4},{2,5},{3,6},{4,7},{5,8},{6,9},{7,10},{8,11},{9,12},{10... | collective-permute-start | bytes 147464 | tf_op jit(solution)/shard_map/ppermute | solution.py:13
  54.1 17.6 %collective-permute-start.10 = (f32[32,384]{1,0:T(8,128)S(1)}, f32[32,384]{1,0:T(8,128)S(1)}, u32[]{:S(2)}, u32[]{:S(2)}) collective-permute-start(f32[32,384]{1,0:T(8,128)S(1)} %fusion.87), channel_id=1, source_target_pairs={{0,2},{1,3},{2,4},{3,5},{4,6},{5,7},{6,8},{7,9},{8,10},{9,11},{10,... | collective-permute-start | bytes 147464 | tf_op jit(solution)/shard_map/ppermute | solution.py:13
  56.1 19.4 %collective-permute-start.11 = (f32[32,384]{1,0:T(8,128)S(1)}, f32[32,384]{1,0:T(8,128)S(1)}, u32[]{:S(2)}, u32[]{:S(2)}) collective-permute-start(f32[32,384]{1,0:T(8,128)S(1)} %fusion.87), channel_id=1, source_target_pairs={{0,1},{1,2},{2,3},{3,4},{4,5},{5,6},{6,7},{7,8},{8,9},{9,10},{10,1... | collective-permute-start | bytes 147464 | tf_op jit(solution)/shard_map/ppermute | solution.py:13
  58.4 17.1 %collective-permute-start.12 = (f32[32,384]{1,0:T(8,128)S(1)}, f32[32,384]{1,0:T(8,128)S(1)}, u32[]{:S(2)}, u32[]{:S(2)}) collective-permute-start(f32[32,384]{1,0:T(8,128)S(1)} %fusion.87), channel_id=1, source_target_pairs={{0,63},{1,0},{2,1},{3,2},{4,3},{5,4},{6,5},{7,6},{8,7},{9,8},{10,9... | collective-permute-start | bytes 147464 | tf_op jit(solution)/shard_map/ppermute | solution.py:13
  86.8 15.9 %collective-permute-start.16 = (f32[32,384]{1,0:T(8,128)S(1)}, f32[32,384]{1,0:T(8,128)S(1)}, u32[]{:S(2)}, u32[]{:S(2)}) collective-permute-start(f32[32,384]{1,0:T(8,128)S(1)} %fusion.86), channel_id=1, source_target_pairs={{0,4},{1,5},{2,6},{3,7},{4,8},{5,9},{6,10},{7,11},{8,12},{9,13},{1... | collective-permute-start | bytes 147464 | tf_op jit(solution)/shard_map/ppermute | solution.py:13
  89.6 16.7 %collective-permute-start.17 = (f32[32,384]{1,0:T(8,128)S(1)}, f32[32,384]{1,0:T(8,128)S(1)}, u32[]{:S(2)}, u32[]{:S(2)}) collective-permute-start(f32[32,384]{1,0:T(8,128)S(1)} %fusion.86), channel_id=1, source_target_pairs={{0,3},{1,4},{2,5},{3,6},{4,7},{5,8},{6,9},{7,10},{8,11},{9,12},{10... | collective-permute-start | bytes 147464 | tf_op jit(solution)/shard_map/ppermute | solution.py:13
  91.5 17.6 %collective-permute-start.18 = (f32[32,384]{1,0:T(8,128)S(1)}, f32[32,384]{1,0:T(8,128)S(1)}, u32[]{:S(2)}, u32[]{:S(2)}) collective-permute-start(f32[32,384]{1,0:T(8,128)S(1)} %fusion.86), channel_id=1, source_target_pairs={{0,2},{1,3},{2,4},{3,5},{4,6},{5,7},{6,8},{7,9},{8,10},{9,11},{10,... | collective-permute-start | bytes 147464 | tf_op jit(solution)/shard_map/ppermute | solution.py:13
  93.9 20.5 %collective-permute-start.19 = (f32[32,384]{1,0:T(8,128)S(1)}, f32[32,384]{1,0:T(8,128)S(1)}, u32[]{:S(2)}, u32[]{:S(2)}) collective-permute-start(f32[32,384]{1,0:T(8,128)S(1)} %fusion.86), channel_id=1, source_target_pairs={{0,1},{1,2},{2,3},{3,4},{4,5},{5,6},{6,7},{7,8},{8,9},{9,10},{10,1... | collective-permute-start | bytes 147464 | tf_op jit(solution)/shard_map/ppermute | solution.py:13
  96.0 18.3 %collective-permute-start.20 = (f32[32,384]{1,0:T(8,128)S(1)}, f32[32,384]{1,0:T(8,128)S(1)}, u32[]{:S(2)}, u32[]{:S(2)}) collective-permute-start(f32[32,384]{1,0:T(8,128)S(1)} %fusion.86), channel_id=1, source_target_pairs={{0,63},{1,0},{2,1},{3,2},{4,3},{5,4},{6,5},{7,6},{8,7},{9,8},{10,9... | collective-permute-start | bytes 147464 | tf_op jit(solution)/shard_map/ppermute | solution.py:13
  124.9 15.1 %collective-permute-start.24 = (f32[32,384]{1,0:T(8,128)S(1)}, f32[32,384]{1,0:T(8,128)S(1)}, u32[]{:S(2)}, u32[]{:S(2)}) collective-permute-start(f32[32,384]{1,0:T(8,128)S(1)} %fusion.83), channel_id=1, source_target_pairs={{0,4},{1,5},{2,6},{3,7},{4,8},{5,9},{6,10},{7,11},{8,12},{9,13},{1... | collective-permute-start | bytes 147464 | tf_op jit(solution)/shard_map/ppermute | solution.py:13
  127.3 16.7 %collective-permute-start.25 = (f32[32,384]{1,0:T(8,128)S(1)}, f32[32,384]{1,0:T(8,128)S(1)}, u32[]{:S(2)}, u32[]{:S(2)}) collective-permute-start(f32[32,384]{1,0:T(8,128)S(1)} %fusion.83), channel_id=1, source_target_pairs={{0,3},{1,4},{2,5},{3,6},{4,7},{5,8},{6,9},{7,10},{8,11},{9,12},{10... | collective-permute-start | bytes 147464 | tf_op jit(solution)/shard_map/ppermute | solution.py:13
  129.2 17.6 %collective-permute-start.26 = (f32[32,384]{1,0:T(8,128)S(1)}, f32[32,384]{1,0:T(8,128)S(1)}, u32[]{:S(2)}, u32[]{:S(2)}) collective-permute-start(f32[32,384]{1,0:T(8,128)S(1)} %fusion.83), channel_id=1, source_target_pairs={{0,2},{1,3},{2,4},{3,5},{4,6},{5,7},{6,8},{7,9},{8,10},{9,11},{10,... | collective-permute-start | bytes 147464 | tf_op jit(solution)/shard_map/ppermute | solution.py:13
  131.1 21.2 %collective-permute-start.27 = (f32[32,384]{1,0:T(8,128)S(1)}, f32[32,384]{1,0:T(8,128)S(1)}, u32[]{:S(2)}, u32[]{:S(2)}) collective-permute-start(f32[32,384]{1,0:T(8,128)S(1)} %fusion.83), channel_id=1, source_target_pairs={{0,1},{1,2},{2,3},{3,4},{4,5},{5,6},{6,7},{7,8},{8,9},{9,10},{10,1... | collective-permute-start | bytes 147464 | tf_op jit(solution)/shard_map/ppermute | solution.py:13
  133.3 19.2 %collective-permute-start.28 = (f32[32,384]{1,0:T(8,128)S(1)}, f32[32,384]{1,0:T(8,128)S(1)}, u32[]{:S(2)}, u32[]{:S(2)}) collective-permute-start(f32[32,384]{1,0:T(8,128)S(1)} %fusion.83), channel_id=1, source_target_pairs={{0,63},{1,0},{2,1},{3,2},{4,3},{5,4},{6,5},{7,6},{8,7},{9,8},{10,9... | collective-permute-start | bytes 147464 | tf_op jit(solution)/shard_map/ppermute | solution.py:13
  162.1 15.7 %collective-permute-start.32 = (f32[32,384]{1,0:T(8,128)S(1)}, f32[32,384]{1,0:T(8,128)S(1)}, u32[]{:S(2)}, u32[]{:S(2)}) collective-permute-start(f32[32,384]{1,0:T(8,128)S(1)} %fusion.80), channel_id=1, source_target_pairs={{0,4},{1,5},{2,6},{3,7},{4,8},{5,9},{6,10},{7,11},{8,12},{9,13},{1... | collective-permute-start | bytes 147464 | tf_op jit(solution)/shard_map/ppermute | solution.py:13
  164.7 16.7 %collective-permute-start.33 = (f32[32,384]{1,0:T(8,128)S(1)}, f32[32,384]{1,0:T(8,128)S(1)}, u32[]{:S(2)}, u32[]{:S(2)}) collective-permute-start(f32[32,384]{1,0:T(8,128)S(1)} %fusion.80), channel_id=1, source_target_pairs={{0,3},{1,4},{2,5},{3,6},{4,7},{5,8},{6,9},{7,10},{8,11},{9,12},{10... | collective-permute-start | bytes 147464 | tf_op jit(solution)/shard_map/ppermute | solution.py:13
  166.6 17.6 %collective-permute-start.34 = (f32[32,384]{1,0:T(8,128)S(1)}, f32[32,384]{1,0:T(8,128)S(1)}, u32[]{:S(2)}, u32[]{:S(2)}) collective-permute-start(f32[32,384]{1,0:T(8,128)S(1)} %fusion.80), channel_id=1, source_target_pairs={{0,2},{1,3},{2,4},{3,5},{4,6},{5,7},{6,8},{7,9},{8,10},{9,11},{10,... | collective-permute-start | bytes 147464 | tf_op jit(solution)/shard_map/ppermute | solution.py:13
  168.8 21.6 %collective-permute-start.35 = (f32[32,384]{1,0:T(8,128)S(1)}, f32[32,384]{1,0:T(8,128)S(1)}, u32[]{:S(2)}, u32[]{:S(2)}) collective-permute-start(f32[32,384]{1,0:T(8,128)S(1)} %fusion.80), channel_id=1, source_target_pairs={{0,1},{1,2},{2,3},{3,4},{4,5},{5,6},{6,7},{7,8},{8,9},{9,10},{10,1... | collective-permute-start | bytes 147464 | tf_op jit(solution)/shard_map/ppermute | solution.py:13
  171.2 19.2 %collective-permute-start.36 = (f32[32,384]{1,0:T(8,128)S(1)}, f32[32,384]{1,0:T(8,128)S(1)}, u32[]{:S(2)}, u32[]{:S(2)}) collective-permute-start(f32[32,384]{1,0:T(8,128)S(1)} %fusion.80), channel_id=1, source_target_pairs={{0,63},{1,0},{2,1},{3,2},{4,3},{5,4},{6,5},{7,6},{8,7},{9,8},{10,9... | collective-permute-start | bytes 147464 | tf_op jit(solution)/shard_map/ppermute | solution.py:13
  177.8 12.7 %collective-permute-start.37 = (f32[32,384]{1,0:T(8,128)S(1)}, f32[32,384]{1,0:T(8,128)S(1)}, u32[]{:S(2)}, u32[]{:S(2)}) collective-permute-start(f32[32,384]{1,0:T(8,128)S(1)} %fusion.80), channel_id=1, source_target_pairs={{0,62},{1,63},{2,0},{3,1},{4,2},{5,3},{6,4},{7,5},{8,6},{9,7},{10,... | collective-permute-start | bytes 147464 | tf_op jit(solution)/shard_map/ppermute | solution.py:13
  200.0 15.3 %collective-permute-start.40 = (f32[32,384]{1,0:T(8,128)S(1)}, f32[32,384]{1,0:T(8,128)S(1)}, u32[]{:S(2)}, u32[]{:S(2)}) collective-permute-start(f32[32,384]{1,0:T(8,128)S(1)} %fusion.77), channel_id=1, source_target_pairs={{0,4},{1,5},{2,6},{3,7},{4,8},{5,9},{6,10},{7,11},{8,12},{9,13},{1... | collective-permute-start | bytes 147464 | tf_op jit(solution)/shard_map/ppermute | solution.py:13
  202.3 16.7 %collective-permute-start.41 = (f32[32,384]{1,0:T(8,128)S(1)}, f32[32,384]{1,0:T(8,128)S(1)}, u32[]{:S(2)}, u32[]{:S(2)}) collective-permute-start(f32[32,384]{1,0:T(8,128)S(1)} %fusion.77), channel_id=1, source_target_pairs={{0,3},{1,4},{2,5},{3,6},{4,7},{5,8},{6,9},{7,10},{8,11},{9,12},{10... | collective-permute-start | bytes 147464 | tf_op jit(solution)/shard_map/ppermute | solution.py:13
  204.3 17.6 %collective-permute-start.42 = (f32[32,384]{1,0:T(8,128)S(1)}, f32[32,384]{1,0:T(8,128)S(1)}, u32[]{:S(2)}, u32[]{:S(2)}) collective-permute-start(f32[32,384]{1,0:T(8,128)S(1)} %fusion.77), channel_id=1, source_target_pairs={{0,2},{1,3},{2,4},{3,5},{4,6},{5,7},{6,8},{7,9},{8,10},{9,11},{10,... | collective-permute-start | bytes 147464 | tf_op jit(solution)/shard_map/ppermute | solution.py:13
  206.2 21.7 %collective-permute-start.43 = (f32[32,384]{1,0:T(8,128)S(1)}, f32[32,384]{1,0:T(8,128)S(1)}, u32[]{:S(2)}, u32[]{:S(2)}) collective-permute-start(f32[32,384]{1,0:T(8,128)S(1)} %fusion.77), channel_id=1, source_target_pairs={{0,1},{1,2},{2,3},{3,4},{4,5},{5,6},{6,7},{7,8},{8,9},{9,10},{10,1... | collective-permute-start | bytes 147464 | tf_op jit(solution)/shard_map/ppermute | solution.py:13
  208.7 19.2 %collective-permute-start.44 = (f32[32,384]{1,0:T(8,128)S(1)}, f32[32,384]{1,0:T(8,128)S(1)}, u32[]{:S(2)}, u32[]{:S(2)}) collective-permute-start(f32[32,384]{1,0:T(8,128)S(1)} %fusion.77), channel_id=1, source_target_pairs={{0,63},{1,0},{2,1},{3,2},{4,3},{5,4},{6,5},{7,6},{8,7},{9,8},{10,9... | collective-permute-start | bytes 147464 | tf_op jit(solution)/shard_map/ppermute | solution.py:13
  215.3 12.7 %collective-permute-start.45 = (f32[32,384]{1,0:T(8,128)S(1)}, f32[32,384]{1,0:T(8,128)S(1)}, u32[]{:S(2)}, u32[]{:S(2)}) collective-permute-start(f32[32,384]{1,0:T(8,128)S(1)} %fusion.77), channel_id=1, source_target_pairs={{0,62},{1,63},{2,0},{3,1},{4,2},{5,3},{6,4},{7,5},{8,6},{9,7},{10,... | collective-permute-start | bytes 147464 | tf_op jit(solution)/shard_map/ppermute | solution.py:13
  237.4 15.7 %collective-permute-start.48 = (f32[32,384]{1,0:T(8,128)S(1)}, f32[32,384]{1,0:T(8,128)S(1)}, u32[]{:S(2)}, u32[]{:S(2)}) collective-permute-start(f32[32,384]{1,0:T(8,128)S(1)} %fusion.74), channel_id=1, source_target_pairs={{0,4},{1,5},{2,6},{3,7},{4,8},{5,9},{6,10},{7,11},{8,12},{9,13},{1... | collective-permute-start | bytes 147464 | tf_op jit(solution)/shard_map/ppermute | solution.py:13
  239.9 16.7 %collective-permute-start.49 = (f32[32,384]{1,0:T(8,128)S(1)}, f32[32,384]{1,0:T(8,128)S(1)}, u32[]{:S(2)}, u32[]{:S(2)}) collective-permute-start(f32[32,384]{1,0:T(8,128)S(1)} %fusion.74), channel_id=1, source_target_pairs={{0,3},{1,4},{2,5},{3,6},{4,7},{5,8},{6,9},{7,10},{8,11},{9,12},{10... | collective-permute-start | bytes 147464 | tf_op jit(solution)/shard_map/ppermute | solution.py:13
  241.9 17.6 %collective-permute-start.50 = (f32[32,384]{1,0:T(8,128)S(1)}, f32[32,384]{1,0:T(8,128)S(1)}, u32[]{:S(2)}, u32[]{:S(2)}) collective-permute-start(f32[32,384]{1,0:T(8,128)S(1)} %fusion.74), channel_id=1, source_target_pairs={{0,2},{1,3},{2,4},{3,5},{4,6},{5,7},{6,8},{7,9},{8,10},{9,11},{10,... | collective-permute-start | bytes 147464 | tf_op jit(solution)/shard_map/ppermute | solution.py:13
  244.2 21.3 %collective-permute-start.51 = (f32[32,384]{1,0:T(8,128)S(1)}, f32[32,384]{1,0:T(8,128)S(1)}, u32[]{:S(2)}, u32[]{:S(2)}) collective-permute-start(f32[32,384]{1,0:T(8,128)S(1)} %fusion.74), channel_id=1, source_target_pairs={{0,1},{1,2},{2,3},{3,4},{4,5},{5,6},{6,7},{7,8},{8,9},{9,10},{10,1... | collective-permute-start | bytes 147464 | tf_op jit(solution)/shard_map/ppermute | solution.py:13
  246.5 19.1 %collective-permute-start.52 = (f32[32,384]{1,0:T(8,128)S(1)}, f32[32,384]{1,0:T(8,128)S(1)}, u32[]{:S(2)}, u32[]{:S(2)}) collective-permute-start(f32[32,384]{1,0:T(8,128)S(1)} %fusion.74), channel_id=1, source_target_pairs={{0,63},{1,0},{2,1},{3,2},{4,3},{5,4},{6,5},{7,6},{8,7},{9,8},{10,9... | collective-permute-start | bytes 147464 | tf_op jit(solution)/shard_map/ppermute | solution.py:13
  275.2 15.4 %collective-permute-start.56 = (f32[32,384]{1,0:T(8,128)S(1)}, f32[32,384]{1,0:T(8,128)S(1)}, u32[]{:S(2)}, u32[]{:S(2)}) collective-permute-start(f32[32,384]{1,0:T(8,128)S(1)} %fusion.71), channel_id=1, source_target_pairs={{0,4},{1,5},{2,6},{3,7},{4,8},{5,9},{6,10},{7,11},{8,12},{9,13},{1... | collective-permute-start | bytes 147464 | tf_op jit(solution)/shard_map/ppermute | solution.py:13
  277.6 16.7 %collective-permute-start.57 = (f32[32,384]{1,0:T(8,128)S(1)}, f32[32,384]{1,0:T(8,128)S(1)}, u32[]{:S(2)}, u32[]{:S(2)}) collective-permute-start(f32[32,384]{1,0:T(8,128)S(1)} %fusion.71), channel_id=1, source_target_pairs={{0,3},{1,4},{2,5},{3,6},{4,7},{5,8},{6,9},{7,10},{8,11},{9,12},{10... | collective-permute-start | bytes 147464 | tf_op jit(solution)/shard_map/ppermute | solution.py:13
  279.6 17.6 %collective-permute-start.58 = (f32[32,384]{1,0:T(8,128)S(1)}, f32[32,384]{1,0:T(8,128)S(1)}, u32[]{:S(2)}, u32[]{:S(2)}) collective-permute-start(f32[32,384]{1,0:T(8,128)S(1)} %fusion.71), channel_id=1, source_target_pairs={{0,2},{1,3},{2,4},{3,5},{4,6},{5,7},{6,8},{7,9},{8,10},{9,11},{10,... | collective-permute-start | bytes 147464 | tf_op jit(solution)/shard_map/ppermute | solution.py:13
  281.6 21.5 %collective-permute-start.59 = (f32[32,384]{1,0:T(8,128)S(1)}, f32[32,384]{1,0:T(8,128)S(1)}, u32[]{:S(2)}, u32[]{:S(2)}) collective-permute-start(f32[32,384]{1,0:T(8,128)S(1)} %fusion.71), channel_id=1, source_target_pairs={{0,1},{1,2},{2,3},{3,4},{4,5},{5,6},{6,7},{7,8},{8,9},{9,10},{10,1... | collective-permute-start | bytes 147464 | tf_op jit(solution)/shard_map/ppermute | solution.py:13
  284.1 19.1 %collective-permute-start.60 = (f32[32,384]{1,0:T(8,128)S(1)}, f32[32,384]{1,0:T(8,128)S(1)}, u32[]{:S(2)}, u32[]{:S(2)}) collective-permute-start(f32[32,384]{1,0:T(8,128)S(1)} %fusion.71), channel_id=1, source_target_pairs={{0,63},{1,0},{2,1},{3,2},{4,3},{5,4},{6,5},{7,6},{8,7},{9,8},{10,9... | collective-permute-start | bytes 147464 | tf_op jit(solution)/shard_map/ppermute | solution.py:13
  290.7 12.5 %collective-permute-start.61 = (f32[32,384]{1,0:T(8,128)S(1)}, f32[32,384]{1,0:T(8,128)S(1)}, u32[]{:S(2)}, u32[]{:S(2)}) collective-permute-start(f32[32,384]{1,0:T(8,128)S(1)} %fusion.71), channel_id=1, source_target_pairs={{0,62},{1,63},{2,0},{3,1},{4,2},{5,3},{6,4},{7,5},{8,6},{9,7},{10,... | collective-permute-start | bytes 147464 | tf_op jit(solution)/shard_map/ppermute | solution.py:13
  372.4 17.9 %collective-permute-start.65 = (f32[32,384]{1,0:T(8,128)S(1)}, f32[32,384]{1,0:T(8,128)S(1)}, u32[]{:S(2)}, u32[]{:S(2)}) collective-permute-start(f32[32,384]{1,0:T(8,128)S(1)} %convolution_multiply_fusion), channel_id=1, source_target_pairs={{0,4},{1,5},{2,6},{3,7},{4,8},{5,9},{6,10},{7,11},{8,12},{9,13},{1... | collective-permute-start | bytes 147464 | tf_op jit(solution)/shard_map/ppermute | solution.py:13
  374.6 17.6 %collective-permute-start.66 = (f32[32,384]{1,0:T(8,128)S(1)}, f32[32,384]{1,0:T(8,128)S(1)}, u32[]{:S(2)}, u32[]{:S(2)}) collective-permute-start(f32[32,384]{1,0:T(8,128)S(1)} %convolution_multiply_fusion), channel_id=1, source_target_pairs={{0,3},{1,4},{2,5},{3,6},{4,7},{5,8},{6,9},{7,10},{8,11},{9,12},{10... | collective-permute-start | bytes 147464 | tf_op jit(solution)/shard_map/ppermute | solution.py:13
  376.6 17.5 %collective-permute-start.67 = (f32[32,384]{1,0:T(8,128)S(1)}, f32[32,384]{1,0:T(8,128)S(1)}, u32[]{:S(2)}, u32[]{:S(2)}) collective-permute-start(f32[32,384]{1,0:T(8,128)S(1)} %convolution_multiply_fusion), channel_id=1, source_target_pairs={{0,2},{1,3},{2,4},{3,5},{4,6},{5,7},{6,8},{7,9},{8,10},{9,11},{10,... | collective-permute-start | bytes 147464 | tf_op jit(solution)/shard_map/ppermute | solution.py:13
  381.3 18.6 %collective-permute-start.68 = (f32[32,384]{1,0:T(8,128)S(1)}, f32[32,384]{1,0:T(8,128)S(1)}, u32[]{:S(2)}, u32[]{:S(2)}) collective-permute-start(f32[32,384]{1,0:T(8,128)S(1)} %convolution_multiply_fusion), channel_id=1, source_target_pairs={{0,1},{1,2},{2,3},{3,4},{4,5},{5,6},{6,7},{7,8},{8,9},{9,10},{10,1... | collective-permute-start | bytes 147464 | tf_op jit(solution)/shard_map/ppermute | solution.py:13
  383.2 18.0 %collective-permute-start.69 = (f32[32,384]{1,0:T(8,128)S(1)}, f32[32,384]{1,0:T(8,128)S(1)}, u32[]{:S(2)}, u32[]{:S(2)}) collective-permute-start(f32[32,384]{1,0:T(8,128)S(1)} %convolution_multiply_fusion), channel_id=1, source_target_pairs={{0,63},{1,0},{2,1},{3,2},{4,3},{5,4},{6,5},{7,6},{8,7},{9,8},{10,9... | collective-permute-start | bytes 147464 | tf_op jit(solution)/shard_map/ppermute | solution.py:13
  (27 other events, 294.8 us)
